TPU v7x, 32 devices: a whole 2x2x4 slice. The times are simulated.
32 devices in a mesh: cluster: 16 (over z, x, core), blk: 2 (over y).
Axes of the slice: x: 2, y: 2, z: 4, core: 2. Of those that a mesh axis runs over, the one named last changes fastest.
Arguments:
- coeff: bfloat16 [512, 8, 2048], P('cluster', None, 'blk'), may hold values from -0.375 to 0.375
- intersection: int32 [16, 32], replicated, may hold values from 0 to 511, as said below
- basis_vals: bfloat16 [8192, 256], P(('cluster', 'blk')), may hold values from -6 to 6
- coulomb: bfloat16 [8192, 7, 256], P(('cluster', 'blk')), may hold values from -0.125 to 0.125
- reach: int32 [32], P(('cluster', 'blk')), may hold values from 0 to 3, as said below
Outputs:
- exchange_out: bfloat16 [8192, 2048], P(('cluster', 'blk'))
Inputs may be any that keep to these rules, and one draw needn't show every extreme that they name: `intersection`: each row lists 32 distinct atoms; atom a is owned by cluster a // 32; at most 4 atoms of one row have the same owner, and each row c holds exactly 4 atoms owned by cluster c. `reach`: some block reaches 3 and some block reaches 0.
All inputs are finite; a program needn't handle non-finite values.
Results may differ from a plain program's by a relative error of at most 0.0059.
Values may be sent and summed in bfloat16 or wider, within the bound.
No kernel may reach another device: no remote copies, remote signals or barrier semaphores. Data moves between devices by JAX's collectives and lax.ppermute only.
A program may use at most 64 MiB of HBM per device.

v0:
```python
import jax
import jax.numpy as jnp
from jax import lax
from jax.sharding import PartitionSpec as P


def passed_along(value, axis, steps):
    count = lax.axis_size(axis)
    pairs = [(source, (source + steps) % count) for source in range(count)]
    return lax.ppermute(value, axis, pairs)


def block_term(local_vals, source, coul_tile, within, norm_factor):
    density = (
        lax.dot_general(
            local_vals, source, (((1,), (1,)), ((), ())), preferred_element_type=jnp.float32
        )
        * norm_factor
    )
    masked_tile = jnp.where(
        within, density * coul_tile.astype(jnp.float32), jnp.float32(0.0)
    ).astype(jnp.bfloat16)
    return jnp.dot(masked_tile, source, preferred_element_type=jnp.float32)


def on_device(coeff, intersection, basis_vals, coulomb, reach):
    num_clusters = lax.axis_size("cluster")
    my_cluster = lax.axis_index("cluster")
    atom_count = coeff.shape[0]
    list_len = intersection.shape[1]
    capacity = 2 * list_len // num_clusters
    num_funcs = coeff.shape[1]
    my_columns = coeff.shape[2]
    half_stops = (coulomb.shape[1] - 1) // 2
    owners = intersection // atom_count
    same_owner = owners[:, :, None] == owners[:, None, :]
    earlier = jnp.arange(list_len)[None, :] < jnp.arange(list_len)[:, None]
    slot_rank = jnp.sum(jnp.logical_and(same_owner, earlier[None, :, :]).astype(jnp.int32), axis=2)
    matches = jnp.logical_and(
        (owners == my_cluster)[:, :, None],
        slot_rank[:, :, None] == jnp.arange(capacity)[None, None, :],
    )
    local_atom = intersection - my_cluster * atom_count
    source_rows = jnp.sum(jnp.where(matches, local_atom[:, :, None], 0), axis=1)
    filled = jnp.any(matches, axis=1)
    outgoing = jnp.take(coeff, source_rows.reshape(-1), axis=0)
    outgoing = jnp.where(filled.reshape(-1)[:, None, None], outgoing, jnp.zeros_like(outgoing))
    outgoing = outgoing.reshape(num_clusters, capacity, num_funcs, my_columns)
    incoming = lax.all_to_all(outgoing, "cluster", split_axis=0, concat_axis=0, tiled=True)
    my_owners = lax.dynamic_index_in_dim(owners, my_cluster, 0, keepdims=False)
    my_ranks = lax.dynamic_index_in_dim(slot_rank, my_cluster, 0, keepdims=False)
    positions = my_owners * capacity + my_ranks
    needed = jnp.take(
        incoming.reshape(num_clusters * capacity, num_funcs * my_columns), positions, axis=0
    )
    needed = needed.reshape(list_len * num_funcs, my_columns)
    all_columns = lax.all_gather(needed, "blk", axis=1, tiled=True)

    def convert(values):
        return jnp.dot(values, all_columns, preferred_element_type=jnp.float32).astype(jnp.bfloat16)

    local_vals = convert(basis_vals)
    norm_factor = local_vals.shape[1] ** (-0.5)
    my_reach = reach[0]

    def term(source, offset):
        return block_term(
            local_vals,
            source,
            coulomb[:, offset + half_stops, :],
            abs(offset) <= my_reach,
            norm_factor,
        )

    accumulated = term(local_vals, 0)
    upward = basis_vals
    downward = basis_vals
    for stop_num in range(1, half_stops + 1):
        upward = passed_along(upward, "blk", -1)
        accumulated = accumulated + term(convert(upward), stop_num)
        downward = passed_along(downward, "blk", 1)
        accumulated = accumulated + term(convert(downward), -stop_num)
    return accumulated.astype(jnp.bfloat16)


def solution(mesh):
    return jax.shard_map(
        on_device,
        mesh=mesh,
        in_specs=(
            P("cluster", None, "blk"),
            P(),
            P(("cluster", "blk"), None),
            P(("cluster", "blk"), None, None),
            P(("cluster", "blk")),
        ),
        out_specs=P(("cluster", "blk"), None),
        check_vma=False,
    )
```

profile of v0, /device:TPU:9, one launch (start us, length us, event | category | flops | bytes accessed | tf_op | source)
XLA Modules:
  0.0 91.6 jit_solution(14014058126347180299)
XLA Ops:
  6.5 0.0 copy-start
  6.5 0.8 broadcast_compare_fusion
  7.3 0.7 broadcast_subtract_fusion
  8.0 0.5 convert_reduce_fusion
  8.5 0.2 select_reduce_fusion
  8.6 0.1 copy.8
  8.7 0.2 fusion.54
  8.9 0.1 reshape.131
  9.0 0.1 copy.7
  9.1 0.1 copy.6
  9.2 0.0 copy-done
  9.2 0.6 gather_fusion
  9.8 1.2 %select_select_fusion = bf16[16,4,8,1024]{3,2,1,0:T(8,128)(2,1)} fusion(bf16[16,4,8,1024]{3,2,1,0:T(8,128)(2,1)S(1)} %bitcast.82, pred[16,4]{1,0:T(8,128)(4,1)S(1)} %copy.7, pred[16,4]{1,0:T(8,128)(4,1)S(1)} %copy.6), kind=kLoop, calls=%fused_computation.21 | loop fusion | flops 1048576 | bytes 2097280 | tf_op jit(solution)/shard_map/jit(_where)/select_n | solution.py:47
  11.0 6.5 %all-to-all-start = ((bf16[16,4,8,1024]{3,2,1,0:T(8,128)(2,1)}), bf16[16,4,8,1024]{3,2,1,0:T(8,128)(2,1)S(1)}, u32[]{:S(2)}, u32[]{:S(2)}) async-start(bf16[16,4,8,1024]{3,2,1,0:T(8,128)(2,1)} %select_select_fusion), calls=%async_computation | async-start | bytes 2097152 | tf_op jit(solution)/shard_map/all_to_all | solution.py:49
  17.6 0.0 all-gather.2.cloned.1.call-start
  17.6 0.1 broadcast_in_dim.66
  17.7 0.1 broadcast_in_dim.67
  17.8 24.7 %all-to-all-done = bf16[16,4,8,1024]{3,2,1,0:T(8,128)(2,1)S(1)} async-done(((bf16[16,4,8,1024]{3,2,1,0:T(8,128)(2,1)}), bf16[16,4,8,1024]{3,2,1,0:T(8,128)(2,1)S(1)}, u32[]{:S(2)}, u32[]{:S(2)}) %all-to-all-start) | async-done | bytes 1048608 | tf_op jit(solution)/shard_map/all_to_all | solution.py:49
  42.5 0.6 copy.9
  43.1 0.9 gather_fusion.1
  44.0 0.0 copy-start.5
  44.0 0.2 gather.15
  44.2 0.9 broadcast_select_fusion
  45.1 0.0 all-gather.2.cloned.1.call-update
  45.2 0.0 copy-done.5
  45.2 1.3 %collective-permute-start = (bf16[256,256]{1,0:T(8,128)(2,1)S(1)}, bf16[256,256]{1,0:T(8,128)(2,1)S(1)}, u32[]{:S(2)}, u32[]{:S(2)}) collective-permute-start(bf16[256,256]{1,0:T(8,128)(2,1)S(1)} %copy-done.5), channel_id=1, source_target_pairs={{0,1},{1,0},{2,3},{3,2},{4,5},{5,4},{6,7},{7,6},{8,9},{9,8},{10,11... | collective-permute-start | bytes 393224 | tf_op jit(solution)/shard_map/ppermute | solution.py:10
  46.5 4.3 %collective-permute-done = bf16[256,256]{1,0:T(8,128)(2,1)S(1)} collective-permute-done((bf16[256,256]{1,0:T(8,128)(2,1)S(1)}, bf16[256,256]{1,0:T(8,128)(2,1)S(1)}, u32[]{:S(2)}, u32[]{:S(2)}) %collective-permute-start) | collective-permute-done | bytes 131104 | tf_op jit(solution)/shard_map/ppermute | solution.py:10
  50.7 1.2 %collective-permute-start.1 = (bf16[256,256]{1,0:T(8,128)(2,1)S(1)}, bf16[256,256]{1,0:T(8,128)(2,1)S(1)}, u32[]{:S(2)}, u32[]{:S(2)}) collective-permute-start(bf16[256,256]{1,0:T(8,128)(2,1)S(1)} %collective-permute-done), channel_id=1, source_target_pairs={{0,1},{1,0},{2,3},{3,2},{4,5},{5,4},{6,7},{7,6},{8,9},{9,8},{10,11... | collective-permute-start | bytes 393224 | tf_op jit(solution)/shard_map/ppermute | solution.py:10
  52.7 4.1 %collective-permute-done.1 = bf16[256,256]{1,0:T(8,128)(2,1)S(1)} collective-permute-done((bf16[256,256]{1,0:T(8,128)(2,1)S(1)}, bf16[256,256]{1,0:T(8,128)(2,1)S(1)}, u32[]{:S(2)}, u32[]{:S(2)}) %collective-permute-start.1) | collective-permute-done | bytes 131104 | tf_op jit(solution)/shard_map/ppermute | solution.py:10
  56.7 2.3 %collective-permute-start.2 = (bf16[256,256]{1,0:T(8,128)(2,1)S(1)}, bf16[256,256]{1,0:T(8,128)(2,1)S(1)}, u32[]{:S(2)}, u32[]{:S(2)}) collective-permute-start(bf16[256,256]{1,0:T(8,128)(2,1)S(1)} %collective-permute-done.1), channel_id=1, source_target_pairs={{0,1},{1,0},{2,3},{3,2},{4,5},{5,4},{6,7},{7,6},{8,9},{9,8},{10,11... | collective-permute-start | bytes 393224 | tf_op jit(solution)/shard_map/ppermute | solution.py:10
  59.0 11.4 %all-gather.2.cloned.1.call-done = bf16[256,2048]{1,0:T(8,128)(2,1)} async-done(((bf16[256,1024]{1,0:T(8,128)(2,1)}), bf16[256,2048]{1,0:T(8,128)(2,1)}) %all-gather.2.cloned.1.call-update) | async-done | bytes 1048592 | tf_op jit(solution)/shard_map/all_gather | solution.py:57
  70.4 0.0 copy-start.1
  70.4 1.8 %convolution_convert_fusion.2 = bf16[2048,256]{1,0:T(8,128)(2,1)S(1)} fusion(bf16[256,2048]{1,0:T(8,128)(2,1)} %all-gather.2.cloned.1.call-done, bf16[256,256]{1,0:T(8,128)(2,1)S(1)} %collective-permute-done), kind=kOutput, calls=%fused_computation.11 | convolution fusion | flops 268959744 | bytes 2228224 | tf_op jit(solution)/shard_map/dot_general | solution.py:60
  72.2 0.0 copy-done.1
  72.2 0.0 copy-start.2
  72.2 0.5 convolution_convert_fusion.3
  72.7 0.5 convolution_multiply_fusion.2
  73.2 0.0 copy-done.2
  73.2 3.6 %fusion.4 = f32[256,2048]{1,0:T(8,128)} fusion(bf16[2048,256]{1,0:T(8,128)(2,1)S(1)} %convolution_convert_fusion.3, bf16[256,7,256]{2,0,1:T(8,128)(2,1)} %param.8, pred[]{:T(512)} %bitcast), kind=kOutput, calls=%fused_computation.20 | convolution fusion | flops 537198592 | bytes 5374464 | tf_op jit(solution)/shard_map/dot_general | solution.py:23
  76.8 0.0 copy-start.3
  76.8 0.0 copy-start.4
  76.8 2.6 %convolution_add_fusion.5 = f32[256,2048]{1,0:T(8,128)S(1)} fusion(f32[256,2048]{1,0:T(8,128)} %fusion.4, bf16[2048,256]{1,0:T(8,128)(2,1)} %copy-done.2, f32[256,256]{1,0:T(8,128)S(1)} %convolution_multiply_fusion.2, bf16[256,7,256]{2,0,1:T(8,128)(2,1)} %param.8, pred[]{:T(512)} %bitcast.7), kind=kOutput, calls=%fused_computation.7 | convolution fusion | flops 269221888 | bytes 5636608 | tf_op jit(solution)/shard_map/dot_general | solution.py:23
  79.3 0.0 copy-done.3
  79.4 0.0 copy-done.4
  79.4 0.5 convolution_add_fusion.4
  79.8 0.5 convolution_convert_fusion.1
  80.3 0.5 convolution_multiply_fusion.1
  80.8 0.5 convolution_add_fusion.3
  81.3 0.5 convolution_add_fusion.2
  81.8 0.0 collective-permute-done.2
  81.8 0.5 convolution_convert_fusion
  82.3 0.5 convolution_multiply_fusion
  82.8 0.5 convolution_add_fusion.1
  83.3 1.4 %fusion = bf16[256,2048]{1,0:T(8,128)(2,1)} fusion(f32[256,2048]{1,0:T(8,128)S(1)} %convolution_add_fusion.1, bf16[2048,256]{1,0:T(8,128)(2,1)S(1)} %convolution_convert_fusion, f32[256,256]{1,0:T(8,128)S(1)} %convolution_multiply_fusion, bf16[256,7,256]{2,0,1:T(8,128)(2,1)S(1)} %copy-done.4, pred[]{:T(512)} %bitcast.13), kind=kOutput, calls=%fused_computation.8 | convolution fusion | flops 269746176 | bytes 4587521 | tf_op jit(solution)/shard_map/dot_general | solution.py:23
  (7 shorter events, 0.1 us)
Async XLA Ops:
  6.5 2.7 %copy-start = (bf16[32,8,1024]{2,1,0:T(8,128)(2,1)S(1)}, bf16[32,8,1024]{2,1,0:T(8,128)(2,1)}, u32[]{:S(2)}) copy-start(bf16[32,8,1024]{2,1,0:T(8,128)(2,1)} %param.5) | copy-start | bytes 1572868
  11.0 31.5 %all-to-all-start = ((bf16[16,4,8,1024]{3,2,1,0:T(8,128)(2,1)}), bf16[16,4,8,1024]{3,2,1,0:T(8,128)(2,1)S(1)}, u32[]{:S(2)}, u32[]{:S(2)}) async-start(bf16[16,4,8,1024]{3,2,1,0:T(8,128)(2,1)} %select_select_fusion), calls=%async_computation | async-start | bytes 2097152 | tf_op jit(solution)/shard_map/all_to_all | solution.py:49
  17.6 52.8 %all-gather.2.cloned.1.call-start = ((), (), s32[]{:S(2)}) async-start(), calls=%async_computation.1 | async-start | bytes 1572864 | tf_op jit(solution)/shard_map/all_gather | solution.py:57
  44.0 1.2 %copy-start.5 = (bf16[256,256]{1,0:T(8,128)(2,1)S(1)}, bf16[256,256]{1,0:T(8,128)(2,1)}, u32[]{:S(2)}) copy-start(bf16[256,256]{1,0:T(8,128)(2,1)} %param.7) | copy-start | bytes 393220
  45.2 5.6 %collective-permute-start = (bf16[256,256]{1,0:T(8,128)(2,1)S(1)}, bf16[256,256]{1,0:T(8,128)(2,1)S(1)}, u32[]{:S(2)}, u32[]{:S(2)}) collective-permute-start(bf16[256,256]{1,0:T(8,128)(2,1)S(1)} %copy-done.5), channel_id=1, source_target_pairs={{0,1},{1,0},{2,3},{3,2},{4,5},{5,4},{6,7},{7,6},{8,9},{9,8},{10,11... | collective-permute-start | bytes 393224 | tf_op jit(solution)/shard_map/ppermute | solution.py:10
  50.7 6.0 %collective-permute-start.1 = (bf16[256,256]{1,0:T(8,128)(2,1)S(1)}, bf16[256,256]{1,0:T(8,128)(2,1)S(1)}, u32[]{:S(2)}, u32[]{:S(2)}) collective-permute-start(bf16[256,256]{1,0:T(8,128)(2,1)S(1)} %collective-permute-done), channel_id=1, source_target_pairs={{0,1},{1,0},{2,3},{3,2},{4,5},{5,4},{6,7},{7,6},{8,9},{9,8},{10,11... | collective-permute-start | bytes 393224 | tf_op jit(solution)/shard_map/ppermute | solution.py:10
  56.7 25.1 %collective-permute-start.2 = (bf16[256,256]{1,0:T(8,128)(2,1)S(1)}, bf16[256,256]{1,0:T(8,128)(2,1)S(1)}, u32[]{:S(2)}, u32[]{:S(2)}) collective-permute-start(bf16[256,256]{1,0:T(8,128)(2,1)S(1)} %collective-permute-done.1), channel_id=1, source_target_pairs={{0,1},{1,0},{2,3},{3,2},{4,5},{5,4},{6,7},{7,6},{8,9},{9,8},{10,11... | collective-permute-start | bytes 393224 | tf_op jit(solution)/shard_map/ppermute | solution.py:10
  70.4 1.8 %copy-start.1 = (bf16[256,2048]{1,0:T(8,128)(2,1)S(1)}, bf16[256,2048]{1,0:T(8,128)(2,1)}, u32[]{:S(2)}) copy-start(bf16[256,2048]{1,0:T(8,128)(2,1)} %all-gather.2.cloned.1.call-done) | copy-start | bytes 3145732
  72.2 1.0 %copy-start.2 = (bf16[2048,256]{1,0:T(8,128)(2,1)}, bf16[2048,256]{1,0:T(8,128)(2,1)S(1)}, u32[]{:S(2)}) copy-start(bf16[2048,256]{1,0:T(8,128)(2,1)S(1)} %convolution_convert_fusion.2) | copy-start | bytes 3145732
  76.8 2.6 %copy-start.3 = (bf16[2048,256]{1,0:T(8,128)(2,1)S(1)}, bf16[2048,256]{1,0:T(8,128)(2,1)}, u32[]{:S(2)}) copy-start(bf16[2048,256]{1,0:T(8,128)(2,1)} %copy-done.2) | copy-start | bytes 3145732
  76.8 2.6 %copy-start.4 = (bf16[256,7,256]{2,0,1:T(8,128)(2,1)S(1)}, bf16[256,7,256]{2,0,1:T(8,128)(2,1)}, u32[]{:S(2)}) copy-start(bf16[256,7,256]{2,0,1:T(8,128)(2,1)} %param.8) | copy-start | bytes 2752516
Sparse Core Ops, SparseCore 0:
  45.3 25.0 all-gather.1
where the time goes:
time: 91.9 us; the launch traced here: 91.6 us
  waiting for transfers between devices  44.4 us (48%)
  between operations  14.3 us (16%)
  matrix products  14.2 us (15%)
  starting transfers between devices  11.4 us (12%)
  other arithmetic  4.38 us (5%)
  local copies, waits for them, and re-layouts  2.9 us (3%)
    all_to_all x1, waiting for transfers between devices, on_device(): lax.all_to_all(outgoing, 'cluster', split_axis=0, concat_axis=0, tiled=True)  24.7 us
    all_gather x1, waiting for transfers between devices, on_device(): all_columns = lax.all_gather(needed, 'blk', axis=1, tiled=True)  11.4 us
    dot_general x7, matrix products, block_term(): return jnp.dot(masked_tile, source, preferred_element_type=jnp.float32)  9.46 us
    ppermute x3, waiting for transfers between devices, passed_along(): return lax.ppermute(value, axis, pairs)  8.33 us
    all_to_all x1, starting transfers between devices, on_device(): lax.all_to_all(outgoing, 'cluster', split_axis=0, concat_axis=0, tiled=True)  6.55 us
    ppermute x3, starting transfers between devices, passed_along(): return lax.ppermute(value, axis, pairs)  4.85 us
    dot_general x4, matrix products, convert(): jnp.dot(values, all_columns, preferred_element_type=jnp.float32)  3.26 us
  transfers between devices with their start and end apart: 5, of which 4 were waited for; matrix products, arithmetic and copies ran while one was open for 13% of the time, Pallas kernels for 0%

commit v1 on v0

v1 whole, which is shorter than its diff:
```python
import jax
import jax.numpy as jnp
from jax import lax
from jax.experimental import pallas as pl
from jax.experimental.pallas import tpu as pltpu
from jax.sharding import PartitionSpec as P


def passed_along(value, axis, steps):
    count = lax.axis_size(axis)
    pairs = [(source, (source + steps) % count) for source in range(count)]
    return lax.ppermute(value, axis, pairs)


def split_high_low(value):
    high = value.astype(jnp.bfloat16)
    low = (value - high.astype(jnp.float32)).astype(jnp.bfloat16)
    return high, low


def dot_nn(a, b):
    return lax.dot_general(a, b, (((1,), (0,)), ((), ())), preferred_element_type=jnp.float32)


def dot_nt(a, b):
    return lax.dot_general(a, b, (((1,), (1,)), ((), ())), preferred_element_type=jnp.float32)


def exchange_kernel(num_sources, num_parts, has_gram, *refs):
    offsets = refs[0]
    basis_refs = refs[1 : 1 + num_sources]
    factor_refs = refs[1 + num_sources : 1 + 2 * num_sources]
    rest = refs[1 + 2 * num_sources :]
    if has_gram:
        gram = rest[0][...]
        rest = rest[1:]
        fresh = range(1, num_parts)
    else:
        gram = None
        fresh = range(num_parts)
    part_refs = rest[:num_parts]
    out_ref = rest[num_parts]
    for part in fresh:
        term = dot_nt(part_refs[part][...], part_refs[part][...])
        gram = term if gram is None else gram + term
    gram_high, gram_low = split_high_low(gram)
    own = basis_refs[0][...]
    projected = dot_nn(own, gram_high) + dot_nn(own, gram_low)
    proj_high, proj_low = split_high_low(projected)
    mixed = None
    for source in range(num_sources):
        basis = basis_refs[source][...]
        density = dot_nt(proj_high, basis) + dot_nt(proj_low, basis)
        tile = (density * factor_refs[source][...]).astype(jnp.bfloat16)
        term = dot_nn(tile, basis)
        mixed = term if mixed is None else mixed + term
    mixed_high, mixed_low = split_high_low(mixed)
    for part in range(num_parts):
        values = part_refs[part][...]
        width = values.shape[1]
        result = dot_nn(mixed_high, values) + dot_nn(mixed_low, values)
        start = pl.multiple_of(offsets[part] * width, width)
        out_ref[:, pl.ds(start, width)] = result.astype(out_ref.dtype)


def on_device(coeff, intersection, basis_vals, coulomb, reach):
    num_clusters = lax.axis_size("cluster")
    num_blocks = lax.axis_size("blk")
    my_cluster = lax.axis_index("cluster")
    my_block = lax.axis_index("blk")
    atom_count, num_funcs, my_columns = coeff.shape
    list_len = intersection.shape[1]
    capacity = 2 * list_len // num_clusters
    half_stops = (coulomb.shape[1] - 1) // 2
    points = basis_vals.shape[0]
    norm_factor = (my_columns * num_blocks) ** (-0.5)

    local_atom = intersection - my_cluster * atom_count
    mine = jnp.logical_and(local_atom >= 0, local_atom < atom_count)
    earlier = jnp.arange(list_len)[:, None] < jnp.arange(list_len)[None, :]
    rank = jnp.dot(mine.astype(jnp.bfloat16), earlier.astype(jnp.bfloat16), preferred_element_type=jnp.float32)
    rank = rank.astype(jnp.int32)
    matches = jnp.logical_and(mine[:, None, :], rank[:, None, :] == jnp.arange(capacity)[None, :, None])
    source_rows = jnp.sum(jnp.where(matches, local_atom[:, None, :], 0), axis=2)
    outgoing = coeff.at[source_rows.reshape(-1)].get(mode="promise_in_bounds")
    outgoing = outgoing.reshape(num_clusters, capacity, num_funcs, my_columns)
    incoming = lax.all_to_all(outgoing, "cluster", split_axis=0, concat_axis=0, tiled=True)

    my_row = lax.dynamic_index_in_dim(intersection, my_cluster, 0, keepdims=False)
    my_owners = my_row // atom_count
    same = jnp.logical_and(my_owners[:, None] == my_owners[None, :], earlier.T)
    my_ranks = jnp.sum(same.astype(jnp.int32), axis=1)
    positions = my_owners * capacity + my_ranks
    needed = incoming.reshape(num_clusters * capacity, num_funcs, my_columns)
    needed = needed.at[positions].get(mode="promise_in_bounds")
    needed = needed.reshape(list_len * num_funcs, my_columns)

    by_step = {}
    for offset in range(-half_stops, half_stops + 1):
        by_step.setdefault(offset % num_blocks, []).append(offset)
    steps = sorted(by_step)
    my_reach = reach[0]
    sources = []
    factors = []
    for step in steps:
        sources.append(basis_vals if step == 0 else passed_along(basis_vals, "blk", -step))
        total = jnp.zeros((points, points), jnp.float32)
        for offset in by_step[step]:
            tile = coulomb[:, offset + half_stops, :].astype(jnp.float32)
            total = total + jnp.where(abs(offset) <= my_reach, tile, jnp.float32(0.0))
        factors.append(total * norm_factor)

    if num_blocks == 2:
        other = passed_along(needed, "blk", 1)
        gram = [dot_nt(needed, needed)]
        parts = [needed, other]
        offsets = jnp.stack([my_block, 1 - my_block])
    else:
        gram = []
        parts = [lax.all_gather(needed, "blk", axis=1, tiled=True)]
        offsets = jnp.zeros((1,), jnp.int32)

    vmem = pl.BlockSpec(memory_space=pltpu.VMEM)
    operands = [offsets, *sources, *factors, *gram, *parts]

    def kernel(*refs):
        exchange_kernel(len(sources), len(parts), bool(gram), *refs)

    return pl.pallas_call(
        kernel,
        out_shape=jax.ShapeDtypeStruct((points, my_columns * num_blocks), jnp.bfloat16),
        in_specs=[pl.BlockSpec(memory_space=pltpu.SMEM)] + [vmem] * (len(operands) - 1),
        out_specs=vmem,
        name="exchange",
    )(*operands)


def solution(mesh):
    return jax.shard_map(
        on_device,
        mesh=mesh,
        in_specs=(
            P("cluster", None, "blk"),
            P(),
            P(("cluster", "blk"), None),
            P(("cluster", "blk"), None, None),
            P(("cluster", "blk")),
        ),
        out_specs=P(("cluster", "blk"), None),
        check_vma=False,
    )
```

time: 91.9 us -> 54.5 us (0.59)
  between operations: 14.3 us -> 0.75 us
  matrix products: 14.2 us -> 1.15 us
  waiting for transfers between devices: 44.4 us -> 32.8 us
  Pallas kernels: 0 us -> 4.4 us
  other arithmetic: 4.38 us -> 1.98 us
  starting transfers between devices: 11.4 us -> 9.29 us
  local copies, waits for them, and re-layouts: 2.9 us -> 3.91 us
    dot_general x14 -> x2, matrix products: 14.2 us -> 1.15 us  [the longest x1 1.02 us: dot_nt(): lax.dot_general(a, b, (((1,), (1,)), ((), ())), preferred_element_type=jn...]
    all_gather x1 -> x0, waiting for transfers between devices: 11.4 us -> none  [on_device(): all_columns = lax.all_gather(needed, 'blk', axis=1, tiled=True)]
    pallas_call x0 -> x1, Pallas kernels: none -> 4.4 us  [on_device(): pl.pallas_call(kernel, out_shape=jax.ShapeDtypeStruct((points, my_columns...]
    ppermute x3 -> x2, starting transfers between devices: 4.85 us -> 2.61 us  [passed_along(): return lax.ppermute(value, axis, pairs)]
    select_n x4 -> x3, other arithmetic: 2.11 us -> 0.04 us  [the longest x1 0.02 us: on_device(): needed = needed.at[positions].get(mode='promise_in_bounds')]
    all_to_all x1, waiting for transfers between devices: 24.7 us -> 23.3 us  [on_device(): lax.all_to_all(outgoing, 'cluster', split_axis=0, concat_axis=0, tiled=True)]
    ppermute x3 -> x2, waiting for transfers between devices: 8.33 us -> 9.42 us  [passed_along(): return lax.ppermute(value, axis, pairs)]
    mul x0 -> x1, other arithmetic: none -> 0.99 us  [on_device(): factors.append(total * norm_factor)]
  transfers between devices with their start and end apart: 5 -> 3, of which waited for: 4 -> 2; matrix products, arithmetic and copies ran while one was open for 13% -> 6% of each run, Pallas kernels for 0% -> 0%
where the time goes in v1:
time: 54.5 us; the launch traced here: 54.2 us
  waiting for transfers between devices  32.8 us (60%)
  starting transfers between devices  9.29 us (17%)
  Pallas kernels  4.4 us (8%)
  local copies, waits for them, and re-layouts  3.91 us (7%)
  other arithmetic  1.98 us (4%)
  matrix products  1.15 us (2%)
  between operations  0.75 us (1%)
    all_to_all x1, waiting for transfers between devices, on_device(): lax.all_to_all(outgoing, 'cluster', split_axis=0, concat_axis=0, tiled=True)  23.3 us
    ppermute x2, waiting for transfers between devices, passed_along(): return lax.ppermute(value, axis, pairs)  9.42 us
    all_to_all x1, starting transfers between devices, on_device(): lax.all_to_all(outgoing, 'cluster', split_axis=0, concat_axis=0, tiled=True)  6.68 us
    pallas_call x1, Pallas kernels, on_device(): pl.pallas_call(kernel, out_shape=jax.ShapeDtypeStruct((points, my_columns...  4.4 us
    ppermute x2, starting transfers between devices, passed_along(): return lax.ppermute(value, axis, pairs)  2.61 us
    gather x1, local copies, waits for them, and re-layouts, on_device(): outgoing = coeff.at[source_rows.reshape(-1)].get(mode='promise_in_bounds')  1.58 us
    unnamed x14, local copies, waits for them, and re-layouts  1.56 us
  transfers between devices with their start and end apart: 3, of which 2 were waited for; matrix products, arithmetic and copies ran while one was open for 6% of the time, Pallas kernels for 0%

profile of v1, /device:TPU:9, one launch (start us, length us, event | category | flops | bytes accessed | tf_op | source)
XLA Modules:
  0.0 54.2 jit_solution(13940961223201648470)
XLA Ops:
  0.0 0.0 copy-start
  0.0 0.0 copy-start.6
  0.0 0.8 %copy-done.6 = s32[16,32]{1,0:T(8,128)S(1)} copy-done((s32[16,32]{1,0:T(8,128)S(1)}, s32[16,32]{1,0:T(8,128)}, u32[]{:S(2)}) %copy-start.6) | copy-done | bytes 2072
  0.8 0.1 convolution_convert_fusion
  0.9 0.1 select_reduce_fusion
  1.0 0.1 copy.6
  1.1 0.1 reshape.181
  1.3 0.0 copy-done
  1.3 1.6 %gather_fusion = bf16[64,8,1024]{2,1,0:T(8,128)(2,1)} fusion(bf16[32,8,1024]{2,1,0:T(8,128)(2,1)S(1)} %copy-done, s32[1024]{0:T(1024)S(1)} %pad_clamp_fusion.1), kind=kCustom, calls=%fused_computation | custom fusion | bytes 2097408 | tf_op jit(solution)/shard_map/gather | solution.py:85
  2.8 0.0 copy-start.4
  2.8 6.7 %all-to-all-start = ((bf16[16,4,8,1024]{3,2,1,0:T(8,128)(2,1)}), bf16[16,4,8,1024]{3,2,1,0:T(8,128)(2,1)S(1)}, u32[]{:S(2)}, u32[]{:S(2)}) async-start(bf16[16,4,8,1024]{3,2,1,0:T(8,128)(2,1)} %bitcast.9), calls=%async_computation | async-start | bytes 2097152 | tf_op jit(solution)/shard_map/all_to_all | solution.py:87
  9.5 0.0 copy-done.4
  9.5 0.0 copy-start.2
  9.5 1.3 %collective-permute-start = (bf16[256,256]{1,0:T(8,128)(2,1)S(1)}, bf16[256,256]{1,0:T(8,128)(2,1)S(1)}, u32[]{:S(2)}, u32[]{:S(2)}) collective-permute-start(bf16[256,256]{1,0:T(8,128)(2,1)S(1)} %copy-done.4), channel_id=1, source_target_pairs={{0,1},{1,0},{2,3},{3,2},{4,5},{5,4},{6,7},{7,6},{8,9},{9,8},{10,11... | collective-permute-start | bytes 393224 | tf_op jit(solution)/shard_map/ppermute | solution.py:12
  10.9 0.2 convert_reduce_fusion
  11.1 23.3 %all-to-all-done = bf16[16,4,8,1024]{3,2,1,0:T(8,128)(2,1)S(1)} async-done(((bf16[16,4,8,1024]{3,2,1,0:T(8,128)(2,1)}), bf16[16,4,8,1024]{3,2,1,0:T(8,128)(2,1)S(1)}, u32[]{:S(2)}, u32[]{:S(2)}) %all-to-all-start) | async-done | bytes 1048608 | tf_op jit(solution)/shard_map/all_to_all | solution.py:87
  34.5 0.6 %gather_fusion.1 = bf16[32,8,1024]{2,1,0:T(8,128)(2,1)S(1)} fusion(bf16[64,8,1024]{2,1,0:T(8,128)(2,1)S(1)} %bitcast.44, s32[1024]{0:T(1024)S(1)} %pad_clamp_fusion), kind=kCustom, calls=%fused_computation.1 | custom fusion | bytes 1048704 | tf_op jit(solution)/shard_map/gather | solution.py:95
  35.0 0.0 copy-start.1
  35.0 1.3 %collective-permute-start.1 = (bf16[256,1024]{1,0:T(8,128)(2,1)S(1)}, bf16[256,1024]{1,0:T(8,128)(2,1)S(1)}, u32[]{:S(2)}, u32[]{:S(2)}) collective-permute-start(bf16[256,1024]{1,0:T(8,128)(2,1)S(1)} %bitcast.45), channel_id=1, source_target_pairs={{0,1},{1,0},{2,3},{3,2},{4,5},{5,4},{6,7},{7,6},{8,9},{9,8},{10,11... | collective-permute-start | bytes 1572872 | tf_op jit(solution)/shard_map/ppermute | solution.py:12
  36.4 0.6 %pad_add_fusion.refs_0_ = s32[2]{0:T(128)} fusion(s32[1]{0:T(128)} %bitcast.1, s32[1]{0:T(128)} %bitcast), kind=kLoop, calls=%fused_computation.32 | loop fusion | flops 2 | bytes 16 | tf_op jit(solution)/shard_map/stack | solution.py:117
  37.6 0.0 copy-done.2
  37.6 1.0 %multiply_bitcast_fusion = (f32[256,256]{1,0:T(8,128)}, f32[256,256]{1,0:T(8,128)}) fusion(bf16[256,7,256]{2,0,1:T(8,128)(2,1)S(1)} %copy-done.2, pred[]{:T(512)} %bitcast.6, pred[]{:T(512)} %bitcast.5, pred[]{:T(512)} %bitcast.3, pred[]{:T(512)} %bitcast.2), kind=kLoop, calls=%fused_computation.3 | loop fusion | flops 1376256 | bytes 1441796 | tf_op jit(solution)/shard_map/mul | solution.py:111
  38.6 0.0 copy-done.1
  38.6 1.0 %fusion.5.refs_5_ = f32[256,256]{1,0:T(8,128)} fusion(bf16[32,8,1024]{2,1,0:T(8,128)(2,1)S(1)} %gather_fusion.1), kind=kOutput, calls=%fused_computation.38 | convolution fusion | flops 134217728 | bytes 786432 | tf_op jit(solution)/shard_map/dot_general | solution.py:26
  39.6 0.0 collective-permute-done.refs_2_
  39.6 0.0 copy-start.5
  39.6 9.4 %collective-permute-done.1.refs_7_ = bf16[256,1024]{1,0:T(8,128)(2,1)S(1)} collective-permute-done((bf16[256,1024]{1,0:T(8,128)(2,1)S(1)}, bf16[256,1024]{1,0:T(8,128)(2,1)S(1)}, u32[]{:S(2)}, u32[]{:S(2)}) %collective-permute-start.1) | collective-permute-done | bytes 524320 | tf_op jit(solution)/shard_map/ppermute | solution.py:12
  49.1 0.0 copy-start.3
  49.1 0.0 copy-done.5
  49.1 0.8 %copy-done.3 = bf16[256,1024]{1,0:T(8,128)(2,1)} copy-done((bf16[256,1024]{1,0:T(8,128)(2,1)}, bf16[256,1024]{1,0:T(8,128)(2,1)S(1)}, u32[]{:S(2)}) %copy-start.3) | copy-done | bytes 524312
  49.8 4.4 %exchange.1 = bf16[256,2048]{1,0:T(8,128)(2,1)} custom-call(s32[2]{0:T(128)} %pad_add_fusion.refs_0_, bf16[256,256]{1,0:T(8,128)(2,1)} %refs_1_.1, bf16[256,256]{1,0:T(8,128)(2,1)} %copy-done.5, f32[256,256]{1,0:T(8,128)} %get-tuple-element.8.refs_3_, f32[256,256]{1,0:T(8,128)} %get-tuple-element.7.refs_4_, f32[256,256]{1,0:T(8,128)} %fusion.5.refs_5_, ...), custom_call_target="tpu_custom_call" | custom-call | tf_op jit(solution)/shard_map/exchange/pallas_call | solution.py:129
  (7 shorter events, 0.1 us)
Async XLA Ops:
  0.0 1.3 %copy-start = (bf16[32,8,1024]{2,1,0:T(8,128)(2,1)S(1)}, bf16[32,8,1024]{2,1,0:T(8,128)(2,1)}, u32[]{:S(2)}) copy-start(bf16[32,8,1024]{2,1,0:T(8,128)(2,1)} %param.5) | copy-start | bytes 1572868
  0.0 0.8 %copy-start.6 = (s32[16,32]{1,0:T(8,128)S(1)}, s32[16,32]{1,0:T(8,128)}, u32[]{:S(2)}) copy-start(s32[16,32]{1,0:T(8,128)} %param.6) | copy-start | bytes 6148
  2.8 6.7 %copy-start.4 = (bf16[256,256]{1,0:T(8,128)(2,1)S(1)}, bf16[256,256]{1,0:T(8,128)(2,1)}, u32[]{:S(2)}) copy-start(bf16[256,256]{1,0:T(8,128)(2,1)} %refs_1_.1) | copy-start | bytes 393220
  2.8 31.6 %all-to-all-start = ((bf16[16,4,8,1024]{3,2,1,0:T(8,128)(2,1)}), bf16[16,4,8,1024]{3,2,1,0:T(8,128)(2,1)S(1)}, u32[]{:S(2)}, u32[]{:S(2)}) async-start(bf16[16,4,8,1024]{3,2,1,0:T(8,128)(2,1)} %bitcast.9), calls=%async_computation | async-start | bytes 2097152 | tf_op jit(solution)/shard_map/all_to_all | solution.py:87
  9.5 28.1 %copy-start.2 = (bf16[256,7,256]{2,0,1:T(8,128)(2,1)S(1)}, bf16[256,7,256]{2,0,1:T(8,128)(2,1)}, u32[]{:S(2)}) copy-start(bf16[256,7,256]{2,0,1:T(8,128)(2,1)} %param.8) | copy-start | bytes 2752516
  9.5 30.1 %collective-permute-start = (bf16[256,256]{1,0:T(8,128)(2,1)S(1)}, bf16[256,256]{1,0:T(8,128)(2,1)S(1)}, u32[]{:S(2)}, u32[]{:S(2)}) collective-permute-start(bf16[256,256]{1,0:T(8,128)(2,1)S(1)} %copy-done.4), channel_id=1, source_target_pairs={{0,1},{1,0},{2,3},{3,2},{4,5},{5,4},{6,7},{7,6},{8,9},{9,8},{10,11... | collective-permute-start | bytes 393224 | tf_op jit(solution)/shard_map/ppermute | solution.py:12
  35.0 3.6 %copy-start.1 = (bf16[32,8,1024]{2,1,0:T(8,128)(2,1)}, bf16[32,8,1024]{2,1,0:T(8,128)(2,1)S(1)}, u32[]{:S(2)}) copy-start(bf16[32,8,1024]{2,1,0:T(8,128)(2,1)S(1)} %gather_fusion.1) | copy-start | bytes 1572868
  35.0 14.0 %collective-permute-start.1 = (bf16[256,1024]{1,0:T(8,128)(2,1)S(1)}, bf16[256,1024]{1,0:T(8,128)(2,1)S(1)}, u32[]{:S(2)}, u32[]{:S(2)}) collective-permute-start(bf16[256,1024]{1,0:T(8,128)(2,1)S(1)} %bitcast.45), channel_id=1, source_target_pairs={{0,1},{1,0},{2,3},{3,2},{4,5},{5,4},{6,7},{7,6},{8,9},{9,8},{10,11... | collective-permute-start | bytes 1572872 | tf_op jit(solution)/shard_map/ppermute | solution.py:12
  39.6 9.4 %copy-start.5 = (bf16[256,256]{1,0:T(8,128)(2,1)}, bf16[256,256]{1,0:T(8,128)(2,1)S(1)}, u32[]{:S(2)}) copy-start(bf16[256,256]{1,0:T(8,128)(2,1)S(1)} %collective-permute-done.refs_2_) | copy-start | bytes 393220
  49.1 0.8 %copy-start.3 = (bf16[256,1024]{1,0:T(8,128)(2,1)}, bf16[256,1024]{1,0:T(8,128)(2,1)S(1)}, u32[]{:S(2)}) copy-start(bf16[256,1024]{1,0:T(8,128)(2,1)S(1)} %collective-permute-done.1.refs_7_) | copy-start | bytes 1572868
